TPU v7x, 32 devices: a whole 2x2x4 slice. The times are simulated.
32 devices in a mesh: frames: 4 (over y, core), win: 8 (over z, x).
Axes of the slice: x: 2, y: 2, z: 4, core: 2. Of those that a mesh axis runs over, the one named last changes fastest.
Arguments:
- memberships: float32 [8, 256, 4096], P('win', 'frames'), as said below
- lag_times: int32 [8], P('win'), may hold values from 1 to 8, as said below
- segment_ids: int32 [8, 256], P('win'), may hold values from 0 to 7, never falling along the last dimension, each value on 1 to 128 neighbouring positions
- bias_codes: int32 [8, 4096], P('win'), may hold values from 0 to 511
Outputs:
- free_energy: float32 [4096], P('frames')
- log_multipliers: float32 [8, 4096], P('win', 'frames')
Inputs may be any that keep to these rules, and one draw needn't show every extreme that they name: Positive; each frame's memberships sum to one up to rounding. `lag_times`: some window's lag time is 8.
All inputs are finite; a program needn't handle non-finite values.
Results may differ from a plain program's by a relative error of at most 0.00041.
Values may be sent and summed in bfloat16 or wider, within the bound.
No kernel may reach another device: no remote copies, remote signals or barrier semaphores. Data moves between devices by JAX's collectives and lax.ppermute only.
A program may use at most 64 MiB of HBM per device.

v0:
```python
import jax
import jax.numpy as jnp
from jax import lax
from jax.sharding import PartitionSpec as P

LAGMAX = 8
ITERS = 2
bias_unit = 1.0 / 128.0


def shifted(block, axis, distance):
    devices = range(lax.axis_size(axis))
    route = [(i - distance, i) for i in devices if i - distance in devices]
    return lax.ppermute(block, axis, route)


def split_rows(block, frames_dev, lag_time, valid_all):
    width = frames_dev + LAGMAX
    number = block.shape[0] // width
    states = block.shape[1]
    shaped = block.reshape(number, width, states)
    current = shaped[:, :frames_dev].reshape(number * frames_dev, states)
    later = lax.dynamic_slice_in_dim(shaped, lag_time, frames_dev, 1).reshape(
        number * frames_dev, states
    )
    later = jnp.where(valid_all[:, None], later, jnp.zeros((), later.dtype))
    return (current, later)


def add_pair(accumulated, current, later, first, rows):
    current_cols = lax.dynamic_slice_in_dim(current, first, rows, 1)
    later_cols = lax.dynamic_slice_in_dim(later, first, rows, 1)
    accumulated = jnp.einsum("tr,ts->rs", current_cols, later, preferred_element_type=jnp.float32)
    return accumulated + jnp.einsum(
        "tr,ts->rs", later_cols, current, preferred_element_type=jnp.float32
    )


def shards(memberships, lag_times, segment_ids, bias_codes):
    member = memberships[0].astype(jnp.bfloat16)
    lag_time = lag_times[0]
    segment_row = segment_ids[0]
    frames_dev = member.shape[0]
    states = member.shape[1]
    frames_all = segment_row.shape[0]
    rows = states // lax.axis_size("frames")
    position = lax.axis_index("frames")
    first = position * rows
    heading = shifted(member[:LAGMAX], "frames", -1)
    extended = jnp.concatenate([member, heading], axis=0)
    segment_ext = jnp.concatenate([segment_row, jnp.full((LAGMAX,), -1, jnp.int32)])
    valid_all = segment_row == lax.dynamic_slice_in_dim(segment_ext, lag_time, frames_all, 0)
    empty = jnp.zeros((rows, states), jnp.float32)
    current, later = split_rows(
        lax.all_gather(extended, "frames", axis=0, tiled=True), frames_dev, lag_time, valid_all
    )
    sym_counts = add_pair(empty, current, later, first, rows)
    gammas = jnp.exp(-bias_codes[0].astype(jnp.float32) * bias_unit)
    gamma_rows = lax.dynamic_slice_in_dim(gammas, first, rows, 0)
    mult_rows = jnp.sum(sym_counts, axis=1) * 0.5
    mult_full = lax.all_gather(mult_rows, "frames", axis=0, tiled=True)
    window_total = jnp.sum(mult_full)
    count_rows = lax.psum(mult_rows, "win")
    weights = jnp.full((states,), 1.0 / states, jnp.float32)
    for sweep in range(ITERS):
        scaled = gammas * weights
        scaled_rows = lax.dynamic_slice_in_dim(scaled, first, rows, 0)
        denom = mult_rows[:, None] * scaled[None, :] + scaled_rows[:, None] * mult_full[None, :]
        ratios = sym_counts / denom
        new_rows = mult_rows * jnp.sum(ratios * scaled[None, :], axis=1)
        terms = gamma_rows * jnp.sum(ratios * mult_full[None, :], axis=1)
        term_rows = lax.psum(terms, "win")
        raw_rows = count_rows / term_rows
        if sweep + 1 < ITERS:
            raw_full, mult_full = (
                lax.all_gather(raw_rows, "frames", axis=0, tiled=True),
                lax.all_gather(new_rows, "frames", axis=0, tiled=True),
            )
        else:
            raw_full = lax.all_gather(raw_rows, "frames", axis=0, tiled=True)
        weights = raw_full / jnp.sum(raw_full)
        mult_rows = new_rows
    weight_rows = lax.dynamic_slice_in_dim(weights, first, rows, 0)
    free_energy = -jnp.log(states * weight_rows)
    log_multipliers = jnp.log(mult_rows * states / window_total)[None, :]
    return (free_energy, log_multipliers)


def solution(mesh):
    placed = (P("win", "frames", None), P("win"), P("win", None), P("win", None))
    return jax.shard_map(
        shards,
        mesh=mesh,
        in_specs=placed,
        out_specs=(P("frames"), P("win", "frames")),
        check_vma=False,
    )
```

profile of v0, /device:TPU:0, one launch (start us, length us, event | category | flops | bytes accessed | tf_op | source)
XLA Modules:
  0.0 147.7 jit_solution(16507466639481832255)
XLA Ops:
  7.2 0.0 all-gather.2.cloned.1.call-start
  7.2 1.3 convert_element_type.11
  8.5 1.3 collective-permute-start
  9.8 1.3 convert_bitcast_fusion
  11.1 0.6 collective-permute-done
  11.7 0.9 pad_maximum_fusion
  12.5 0.0 all-gather.2.cloned.1.call-update
  13.2 0.8 broadcast_multiply_fusion
  14.0 0.8 fusion.6
  14.8 25.7 %all-gather.2.cloned.1.call-done = bf16[288,4096]{1,0:T(8,128)(2,1)} async-done(((bf16[72,4096]{1,0:T(8,128)(2,1)}), bf16[288,4096]{1,0:T(8,128)(2,1)}) %all-gather.2.cloned.1.call-update) | async-done | bytes 2359312 | tf_op jit(solution)/shard_map/all_gather | solution.py:55
  40.5 2.9 %fusion.10 = (bf16[4,64,4096]{2,1,0:T(8,128)(2,1)S(1)}, bf16[4,64,4096]{2,1,0:T(8,128)(2,1)S(1)}) fusion(bf16[4,72,4096]{2,1,0:T(8,128)(2,1)} %bitcast.23, s32[]{:T(128)S(6)} %select_n.20), kind=kLoop, calls=%fused_computation.30 | loop fusion | bytes 8388612 | tf_op jit(solution)/shard_map/slice | solution.py:22
  43.4 0.0 copy-start.1
  43.4 0.4 bitcast_select_fusion
  43.8 0.9 copy-done.1
  44.8 8.1 %fusion.1 = f32[1024,4096]{1,0:T(8,128)} fusion(bf16[256,4096]{1,0:T(8,128)(2,1)S(1)} %bitcast_select_fusion, bf16[256,4096]{1,0:T(8,128)(2,1)S(1)} %bitcast.21, s32[]{:T(128)S(6)} %select_n.18), kind=kOutput, calls=%fused_computation.10 | convolution fusion | flops 2147483648 | bytes 19398660 | tf_op jit(solution)/shard_map/tr,ts->rs/dot_general | solution.py:33
  52.9 7.8 %fusion.11 = (f32[1024]{0:T(1024)S(1)}, f32[1024,4096]{1,0:T(8,128)S(1)}) fusion(f32[1024,4096]{1,0:T(8,128)} %fusion.1, bf16[256,4096]{1,0:T(8,128)(2,1)} %bitcast.22, bf16[256,4096]{1,0:T(8,128)(2,1)S(1)} %bitcast_select_fusion, s32[]{:T(128)S(6)} %select_n.18), kind=kOutput, calls=%fused_computation.31 | convolution fusion | flops 2155871232 | bytes 36179972 | tf_op jit(solution)/shard_map/tr,ts->rs/dot_general | solution.py:34
  60.7 0.0 copy-start
  60.7 5.2 %all_gather.16 = f32[4096]{0:T(1024)S(1)} all-gather(f32[1024]{0:T(1024)S(1)} %broadcast_multiply_fusion.1), channel_id=1, replica_groups=mesh['frames'=4,'win'=8] {'frames'}, dimensions={0}, use_global_device_ids=true | all-gather | bytes 20480 | tf_op jit(solution)/shard_map/all_gather | solution.py:61
  65.9 0.5 copy-done
  66.4 6.2 %multiply_reduce_fusion.2 = (f32[1024]{0:T(1024)S(1)}, f32[1024]{0:T(1024)S(1)}) fusion(f32[4096]{0:T(1024)S(1)} %all_gather.16, f32[4096]{0:T(1024)S(1)} %bitcast.26, f32[1024,4096]{1,0:T(8,128)S(1)} %get-tuple-element.13, f32[1024]{0:T(1024)S(1)} %dynamic-slice_multiply_fusion, f32[1024]{0:T(1024)S(1)} %broadcast_multiply_fusion.1), kind=kLoop, calls=%fused_computation.3 | loop fusion | flops 33552384 | bytes 16826368 | tf_op jit(solution)/shard_map/reduce_sum | solution.py:71
  72.6 5.2 %all_gather.18 = f32[4096]{0:T(1024)S(1)} all-gather(f32[1024]{0:T(1024)S(1)} %fusion.9), channel_id=1, replica_groups=mesh['frames'=4,'win'=8] {'frames'}, dimensions={0}, use_global_device_ids=true | all-gather | bytes 20480 | tf_op jit(solution)/shard_map/all_gather | solution.py:77
  77.8 21.6 %all-reduce.1 = (f32[1024]{0:T(1024)S(1)}, f32[1024]{0:T(1024)S(1)}) all-reduce(f32[1024]{0:T(1024)S(1)} %broadcast_multiply_fusion.1, f32[1024]{0:T(1024)S(1)} %mul.185), channel_id=1, replica_groups=mesh['frames'=4,'win'=8] {'win'}, use_global_device_ids=true, to_apply=%region_1.2 | all-reduce | flops 2048 | bytes 16384 | tf_op jit(solution)/shard_map/psum | solution.py:63
  99.4 5.2 %all_gather.17 = f32[4096]{0:T(1024)S(1)} all-gather(f32[1024]{0:T(1024)S(1)} %div.38), channel_id=1, replica_groups=mesh['frames'=4,'win'=8] {'frames'}, dimensions={0}, use_global_device_ids=true | all-gather | bytes 20480 | tf_op jit(solution)/shard_map/all_gather | solution.py:76
  104.6 0.6 reduce_sum.79
  105.2 0.6 reduce_sum.75
  105.8 0.7 divide_multiply_fusion
  106.5 9.0 %multiply_reduce_fusion = (f32[1024]{0:T(1024)S(1)}, f32[1024]{0:T(1024)S(1)}) fusion(f32[4096]{0:T(1024)S(1)} %divide_multiply_fusion, f32[4096]{0:T(1024)S(1)} %all_gather.18, f32[1024,4096]{1,0:T(8,128)} %copy-done, f32[1024]{0:T(1024)S(1)} %dynamic_slice.33, f32[1024]{0:T(1024)S(1)} %fusion.9), kind=kLoop, calls=%fused_computation | loop fusion | flops 33552384 | bytes 16826368 | tf_op jit(solution)/shard_map/reduce_sum | solution.py:70
  115.5 17.1 %psum.23 = f32[1024]{0:T(1024)S(1)} all-reduce(f32[1024]{0:T(1024)S(1)} %mul.193), channel_id=1, replica_groups=mesh['frames'=4,'win'=8] {'win'}, use_global_device_ids=true, to_apply=%region_7.8 | all-reduce | flops 1024 | bytes 8192 | tf_op jit(solution)/shard_map/psum | solution.py:72
  132.7 5.2 %all_gather.19 = f32[4096]{0:T(1024)S(1)} all-gather(f32[1024]{0:T(1024)S(1)} %div.42), channel_id=1, replica_groups=mesh['frames'=4,'win'=8] {'frames'}, dimensions={0}, use_global_device_ids=true | all-gather | bytes 20480 | tf_op jit(solution)/shard_map/all_gather | solution.py:80
  137.9 0.6 reduce_sum.77
  138.5 1.3 fusion.5
  139.7 1.2 divide_log_fusion
  (10 shorter events, 0.1 us)
Async XLA Ops:
  7.2 33.3 %all-gather.2.cloned.1.call-start = ((), (), s32[]{:S(2)}) async-start(), calls=%async_computation | async-start | bytes 2949120 | tf_op jit(solution)/shard_map/all_gather | solution.py:55
  8.5 3.1 %collective-permute-start = (bf16[8,4096]{1,0:T(8,128)(2,1)S(1)}, bf16[8,4096]{1,0:T(8,128)(2,1)S(1)}, u32[]{:S(2)}, u32[]{:S(2)}) collective-permute-start(bf16[8,4096]{1,0:T(8,128)(2,1)S(1)} %slice_bitcast_fusion), channel_id=1, source_target_pairs={{8,0},{16,8},{24,16},{9,1},{17,9},{25,17},{10,2},{18,10},{26,18},{... | collective-permute-start | bytes 196616 | tf_op jit(solution)/shard_map/ppermute | solution.py:14
  43.4 1.4 copy-start.1
  60.7 5.7 %copy-start = (f32[1024,4096]{1,0:T(8,128)}, f32[1024,4096]{1,0:T(8,128)S(1)}, u32[]{:S(2)}) copy-start(f32[1024,4096]{1,0:T(8,128)S(1)} %get-tuple-element.13) | copy-start | bytes 50331652
Sparse Core Ops, SparseCore 0:
  12.7 27.7 all-gather.1
where the time goes:
time: 148 us
  blocking collectives  59.6 us (40%)
  waiting for transfers between devices  26.2 us (18%)
  other arithmetic  25.5 us (17%)
  matrix products  15.9 us (11%)
  between operations  14.8 us (10%)
  local copies, waits for them, and re-layouts  4.38 us (3%)
    all_gather x1, waiting for transfers between devices, shards(): lax.all_gather(extended, 'frames', axis=0, tiled=True)  25.7 us
    psum x1, blocking collectives, shards(): count_rows = lax.psum(mult_rows, 'win')  21.6 us
    psum x1, blocking collectives, shards(): term_rows = lax.psum(terms, 'win')  17.1 us
    reduce_sum x1, other arithmetic, shards(): new_rows = mult_rows * jnp.sum(ratios * scaled[None, :], axis=1)  8.98 us
    dot_general x1, matrix products, add_pair(): jnp.einsum('tr,ts->rs', current_cols, later, preferred_element_type=jnp.f...  8.12 us
    dot_general x1, matrix products, add_pair(): jnp.einsum('tr,ts->rs', later_cols, current, preferred_element_type=jnp.f...  7.76 us
    reduce_sum x1, other arithmetic, shards(): terms = gamma_rows * jnp.sum(ratios * mult_full[None, :], axis=1)  6.19 us
    all_gather x1, blocking collectives, shards(): mult_full = lax.all_gather(mult_rows, 'frames', axis=0, tiled=True)  5.21 us
  transfers between devices with their start and end apart: 2, of which 2 were waited for; matrix products, arithmetic and copies ran while one was open for 2% of the time, Pallas kernels for 0%

commit v1 on v0

--- a/solution.py
+++ b/solution.py
@@ -6,6 +6,19 @@
 LAGMAX = 8
 ITERS = 2
 bias_unit = 1.0 / 128.0
+
+
+def gather_around(x, axis, dim):
+    ways = lax.axis_size(axis)
+    up = [(d, (d + 1) % ways) for d in range(ways)]
+    down = [(d, (d - 1) % ways) for d in range(ways)]
+    earlier, later = ([x], [x])
+    for _ in range(ways // 2):
+        earlier.append(lax.ppermute(earlier[-1], axis, up))
+    for _ in range((ways - 1) // 2):
+        later.append(lax.ppermute(later[-1], axis, down))
+    line = jnp.concatenate([*earlier[::-1], *later[1:]], axis=dim)
+    return jnp.roll(line, (lax.axis_index(axis) - ways // 2) * x.shape[dim], axis=dim)
 
 
 def shifted(block, axis, distance):
@@ -52,7 +65,7 @@
     valid_all = segment_row == lax.dynamic_slice_in_dim(segment_ext, lag_time, frames_all, 0)
     empty = jnp.zeros((rows, states), jnp.float32)
     current, later = split_rows(
-        lax.all_gather(extended, "frames", axis=0, tiled=True), frames_dev, lag_time, valid_all
+        gather_around(extended, "frames", 0), frames_dev, lag_time, valid_all
     )
     sym_counts = add_pair(empty, current, later, first, rows)
     gammas = jnp.exp(-bias_codes[0].astype(jnp.float32) * bias_unit)

time: 148 us -> 131 us (0.89)
  between operations: 14.8 us -> 1.57 us
  waiting for transfers between devices: 26.2 us -> 18.7 us
  starting transfers between devices: 1.33 us -> 6.9 us
  local copies, waits for them, and re-layouts: 4.38 us -> 2.52 us
    all_gather x1 -> x0, waiting for transfers between devices: 25.7 us -> none  [shards(): lax.all_gather(extended, 'frames', axis=0, tiled=True)]
    ppermute x0 -> x3, waiting for transfers between devices: none -> 18.1 us  [the longest x2 13.6 us: gather_around(): earlier.append(lax.ppermute(earlier[-1], axis, up))]
    ppermute x0 -> x3, starting transfers between devices: none -> 5.61 us  [the longest x2 3.87 us: gather_around(): earlier.append(lax.ppermute(earlier[-1], axis, up))]
    slice x1, local copies, waits for them, and re-layouts: 2.92 us -> 0.7 us  [split_rows(): current = shaped[:, :frames_dev].reshape(number * frames_dev, states)]
  transfers between devices with their start and end apart: 2 -> 4, of which waited for: 2 -> 4; matrix products, arithmetic and copies ran while one was open for 2% -> 2% of each run, Pallas kernels for 0% -> 0%
where the time goes in v1:
time: 131 us
  blocking collectives  60.1 us (46%)
  other arithmetic  24.9 us (19%)
  waiting for transfers between devices  18.7 us (14%)
  matrix products  15.9 us (12%)
  starting transfers between devices  6.9 us (5%)
  local copies, waits for them, and re-layouts  2.52 us (2%)
  between operations  1.57 us (1%)
    psum x1, blocking collectives, shards(): count_rows = lax.psum(mult_rows, 'win')  21.9 us
    psum x1, blocking collectives, shards(): term_rows = lax.psum(terms, 'win')  17.1 us
    ppermute x2, waiting for transfers between devices, gather_around(): earlier.append(lax.ppermute(earlier[-1], axis, up))  13.6 us
    reduce_sum x1, other arithmetic, shards(): new_rows = mult_rows * jnp.sum(ratios * scaled[None, :], axis=1)  8.98 us
    dot_general x1, matrix products, add_pair(): jnp.einsum('tr,ts->rs', current_cols, later, preferred_element_type=jnp.f...  8.12 us
    dot_general x1, matrix products, add_pair(): jnp.einsum('tr,ts->rs', later_cols, current, preferred_element_type=jnp.f...  7.77 us
    reduce_sum x1, other arithmetic, shards(): terms = gamma_rows * jnp.sum(ratios * mult_full[None, :], axis=1)  6.19 us
    all_gather x1, blocking collectives, shards(): mult_full = lax.all_gather(mult_rows, 'frames', axis=0, tiled=True)  5.46 us
  transfers between devices with their start and end apart: 4, of which 4 were waited for; matrix products, arithmetic and copies ran while one was open for 2% of the time, Pallas kernels for 0%

profile of v1, /device:TPU:0, one launch (start us, length us, event | category | flops | bytes accessed | tf_op | source)
XLA Modules:
  0.0 130.5 jit_solution(14376216983690428754)
XLA Ops:
  0.6 0.0 copy-start.1
  0.6 1.4 %convert_element_type.11 = bf16[1,64,4096]{2,1,0:T(8,128)(2,1)S(1)} convert(f32[1,64,4096]{2,1,0:T(8,128)} %param.4) | non-fusion elementwise | flops 262144 | bytes 1572864 | tf_op jit(solution)/shard_map/convert_element_type | solution.py:53
  2.0 1.3 collective-permute-start
  3.3 1.3 convert_bitcast_fusion
  4.6 0.6 collective-permute-done
  5.2 3.9 %collective-permute-start.1 = (bf16[72,4096]{1,0:T(8,128)(2,1)S(1)}, bf16[72,4096]{1,0:T(8,128)(2,1)S(1)}, u32[]{:S(2)}, u32[]{:S(2)}) collective-permute-start(bf16[72,4096]{1,0:T(8,128)(2,1)S(1)} %pad_maximum_fusion), channel_id=1, source_target_pairs={{0,8},{8,16},{16,24},{24,0},{1,9},{9,17},{17,25},{25,1},{2,10},{10... | collective-permute-start | bytes 1769480 | tf_op jit(solution)/shard_map/ppermute | solution.py:17
  9.1 6.9 %collective-permute-done.1 = bf16[72,4096]{1,0:T(8,128)(2,1)S(1)} collective-permute-done((bf16[72,4096]{1,0:T(8,128)(2,1)S(1)}, bf16[72,4096]{1,0:T(8,128)(2,1)S(1)}, u32[]{:S(2)}, u32[]{:S(2)}) %collective-permute-start.1) | collective-permute-done | bytes 589856 | tf_op jit(solution)/shard_map/ppermute | solution.py:17
  16.0 0.0 collective-permute-start.2
  16.0 0.7 broadcast_multiply_fusion
  17.5 0.8 fusion.8
  18.3 1.7 %collective-permute-start.3 = (bf16[72,4096]{1,0:T(8,128)(2,1)S(1)}, bf16[72,4096]{1,0:T(8,128)(2,1)S(1)}, u32[]{:S(2)}, u32[]{:S(2)}) collective-permute-start(bf16[72,4096]{1,0:T(8,128)(2,1)S(1)} %pad_maximum_fusion), channel_id=1, source_target_pairs={{0,24},{8,0},{16,8},{24,16},{1,25},{9,1},{17,9},{25,17},{2,26},{10... | collective-permute-start | bytes 1769480 | tf_op jit(solution)/shard_map/ppermute | solution.py:19
  20.1 6.7 %collective-permute-done.2 = bf16[72,4096]{1,0:T(8,128)(2,1)S(1)} collective-permute-done((bf16[72,4096]{1,0:T(8,128)(2,1)S(1)}, bf16[72,4096]{1,0:T(8,128)(2,1)S(1)}, u32[]{:S(2)}, u32[]{:S(2)}) %collective-permute-start.2) | collective-permute-done | bytes 589856 | tf_op jit(solution)/shard_map/ppermute | solution.py:17
  26.9 0.0 copy-done.1
  26.9 0.1 constant_dynamic-update-slice_fusion.7
  26.9 4.5 %collective-permute-done.3 = bf16[72,4096]{1,0:T(8,128)(2,1)S(1)} collective-permute-done((bf16[72,4096]{1,0:T(8,128)(2,1)S(1)}, bf16[72,4096]{1,0:T(8,128)(2,1)S(1)}, u32[]{:S(2)}, u32[]{:S(2)}) %collective-permute-start.3) | collective-permute-done | bytes 589856 | tf_op jit(solution)/shard_map/ppermute | solution.py:19
  31.6 0.1 constant_dynamic-update-slice_fusion.2
  31.7 0.6 constant_dynamic-slice_fusion.2
  32.3 0.7 fusion.10
  33.0 0.0 copy-start.2
  33.0 0.4 bitcast_select_fusion
  33.4 0.9 copy-done.2
  34.4 8.1 %fusion.1 = f32[1024,4096]{1,0:T(8,128)} fusion(bf16[256,4096]{1,0:T(8,128)(2,1)S(1)} %bitcast_select_fusion, bf16[256,4096]{1,0:T(8,128)(2,1)S(1)} %bitcast.24, s32[]{:T(128)S(6)} %select_n.33), kind=kOutput, calls=%fused_computation.10 | convolution fusion | flops 2147483648 | bytes 19398660 | tf_op jit(solution)/shard_map/tr,ts->rs/dot_general | solution.py:46
  42.5 7.8 %fusion.11 = (f32[1024]{0:T(1024)S(1)}, f32[1024,4096]{1,0:T(8,128)S(1)}) fusion(f32[1024,4096]{1,0:T(8,128)} %fusion.1, bf16[256,4096]{1,0:T(8,128)(2,1)} %bitcast.25, bf16[256,4096]{1,0:T(8,128)(2,1)S(1)} %bitcast_select_fusion, s32[]{:T(128)S(6)} %select_n.33), kind=kOutput, calls=%fused_computation.42 | convolution fusion | flops 2155871232 | bytes 36179972 | tf_op jit(solution)/shard_map/tr,ts->rs/dot_general | solution.py:47
  50.2 0.0 copy-start
  50.3 5.5 %all_gather.12 = f32[4096]{0:T(1024)S(1)} all-gather(f32[1024]{0:T(1024)S(1)} %broadcast_multiply_fusion.1), channel_id=1, replica_groups=mesh['frames'=4,'win'=8] {'frames'}, dimensions={0}, use_global_device_ids=true | all-gather | bytes 20480 | tf_op jit(solution)/shard_map/all_gather | solution.py:74
  55.7 6.2 %multiply_reduce_fusion.2 = (f32[1024]{0:T(1024)S(1)}, f32[1024]{0:T(1024)S(1)}) fusion(f32[4096]{0:T(1024)S(1)} %all_gather.12, f32[4096]{0:T(1024)S(1)} %bitcast.28, f32[1024,4096]{1,0:T(8,128)S(1)} %get-tuple-element.13, f32[1024]{0:T(1024)S(1)} %dynamic-slice_multiply_fusion, f32[1024]{0:T(1024)S(1)} %broadcast_multiply_fusion.1), kind=kLoop, calls=%fused_computation.3 | loop fusion | flops 33552384 | bytes 16826368 | tf_op jit(solution)/shard_map/reduce_sum | solution.py:84
  61.9 0.0 copy-done
  61.9 5.2 %all_gather.14 = f32[4096]{0:T(1024)S(1)} all-gather(f32[1024]{0:T(1024)S(1)} %fusion.9), channel_id=1, replica_groups=mesh['frames'=4,'win'=8] {'frames'}, dimensions={0}, use_global_device_ids=true | all-gather | bytes 20480 | tf_op jit(solution)/shard_map/all_gather | solution.py:90
  67.2 21.9 %all-reduce.1 = (f32[1024]{0:T(1024)S(1)}, f32[1024]{0:T(1024)S(1)}) all-reduce(f32[1024]{0:T(1024)S(1)} %broadcast_multiply_fusion.1, f32[1024]{0:T(1024)S(1)} %mul.189), channel_id=1, replica_groups=mesh['frames'=4,'win'=8] {'win'}, use_global_device_ids=true, to_apply=%region_1.2 | all-reduce | flops 2048 | bytes 16384 | tf_op jit(solution)/shard_map/psum | solution.py:76
  89.1 5.2 %all_gather.13 = f32[4096]{0:T(1024)S(1)} all-gather(f32[1024]{0:T(1024)S(1)} %div.38), channel_id=1, replica_groups=mesh['frames'=4,'win'=8] {'frames'}, dimensions={0}, use_global_device_ids=true | all-gather | bytes 20480 | tf_op jit(solution)/shard_map/all_gather | solution.py:89
  94.3 0.6 reduce_sum.79
  94.9 0.6 reduce_sum.75
  95.5 0.7 divide_multiply_fusion
  96.1 9.0 %multiply_reduce_fusion = (f32[1024]{0:T(1024)S(1)}, f32[1024]{0:T(1024)S(1)}) fusion(f32[4096]{0:T(1024)S(1)} %divide_multiply_fusion, f32[4096]{0:T(1024)S(1)} %all_gather.14, f32[1024,4096]{1,0:T(8,128)} %copy-done, f32[1024]{0:T(1024)S(1)} %dynamic_slice.38, f32[1024]{0:T(1024)S(1)} %fusion.9), kind=kLoop, calls=%fused_computation | loop fusion | flops 33552384 | bytes 16826368 | tf_op jit(solution)/shard_map/reduce_sum | solution.py:83
  105.1 17.1 %psum.23 = f32[1024]{0:T(1024)S(1)} all-reduce(f32[1024]{0:T(1024)S(1)} %mul.197), channel_id=1, replica_groups=mesh['frames'=4,'win'=8] {'win'}, use_global_device_ids=true, to_apply=%region_7.8 | all-reduce | flops 1024 | bytes 8192 | tf_op jit(solution)/shard_map/psum | solution.py:85
  122.3 5.2 %all_gather.15 = f32[4096]{0:T(1024)S(1)} all-gather(f32[1024]{0:T(1024)S(1)} %div.42), channel_id=1, replica_groups=mesh['frames'=4,'win'=8] {'frames'}, dimensions={0}, use_global_device_ids=true | all-gather | bytes 20480 | tf_op jit(solution)/shard_map/all_gather | solution.py:93
  127.5 0.6 reduce_sum.77
  128.1 1.3 fusion.5
  129.3 1.2 divide_log_fusion
  (19 shorter events, 0.4 us)
Async XLA Ops:
  0.6 26.2 %copy-start.1 = (f32[1,64,4096]{2,1,0:T(8,128)S(1)}, f32[1,64,4096]{2,1,0:T(8,128)}, u32[]{:S(2)}) copy-start(f32[1,64,4096]{2,1,0:T(8,128)} %param.4) | copy-start | bytes 3145732
  2.0 3.1 %collective-permute-start = (bf16[8,4096]{1,0:T(8,128)(2,1)S(1)}, bf16[8,4096]{1,0:T(8,128)(2,1)S(1)}, u32[]{:S(2)}, u32[]{:S(2)}) collective-permute-start(bf16[8,4096]{1,0:T(8,128)(2,1)S(1)} %slice_bitcast_fusion), channel_id=1, source_target_pairs={{8,0},{16,8},{24,16},{9,1},{17,9},{25,17},{10,2},{18,10},{26,18},{... | collective-permute-start | bytes 196616 | tf_op jit(solution)/shard_map/ppermute | solution.py:27
  5.2 10.8 %collective-permute-start.1 = (bf16[72,4096]{1,0:T(8,128)(2,1)S(1)}, bf16[72,4096]{1,0:T(8,128)(2,1)S(1)}, u32[]{:S(2)}, u32[]{:S(2)}) collective-permute-start(bf16[72,4096]{1,0:T(8,128)(2,1)S(1)} %pad_maximum_fusion), channel_id=1, source_target_pairs={{0,8},{8,16},{16,24},{24,0},{1,9},{9,17},{17,25},{25,1},{2,10},{10... | collective-permute-start | bytes 1769480 | tf_op jit(solution)/shard_map/ppermute | solution.py:17
  16.0 10.8 %collective-permute-start.2 = (bf16[72,4096]{1,0:T(8,128)(2,1)S(1)}, bf16[72,4096]{1,0:T(8,128)(2,1)S(1)}, u32[]{:S(2)}, u32[]{:S(2)}) collective-permute-start(bf16[72,4096]{1,0:T(8,128)(2,1)S(1)} %collective-permute-done.1), channel_id=1, source_target_pairs={{0,8},{8,16},{16,24},{24,0},{1,9},{9,17},{17,25},{25,1},{2,10},{10... | collective-permute-start | bytes 1769480 | tf_op jit(solution)/shard_map/ppermute | solution.py:17
  18.3 13.1 %collective-permute-start.3 = (bf16[72,4096]{1,0:T(8,128)(2,1)S(1)}, bf16[72,4096]{1,0:T(8,128)(2,1)S(1)}, u32[]{:S(2)}, u32[]{:S(2)}) collective-permute-start(bf16[72,4096]{1,0:T(8,128)(2,1)S(1)} %pad_maximum_fusion), channel_id=1, source_target_pairs={{0,24},{8,0},{16,8},{24,16},{1,25},{9,1},{17,9},{25,17},{2,26},{10... | collective-permute-start | bytes 1769480 | tf_op jit(solution)/shard_map/ppermute | solution.py:19
  33.0 1.4 %copy-start.2 = (bf16[4,64,4096]{2,1,0:T(8,128)(2,1)}, bf16[4,64,4096]{2,1,0:T(8,128)(2,1)S(1)}, u32[]{:S(2)}) copy-start(bf16[4,64,4096]{2,1,0:T(8,128)(2,1)S(1)} %get-tuple-element.10) | copy-start | bytes 6291460
  50.2 11.7 %copy-start = (f32[1024,4096]{1,0:T(8,128)}, f32[1024,4096]{1,0:T(8,128)S(1)}, u32[]{:S(2)}) copy-start(f32[1024,4096]{1,0:T(8,128)S(1)} %get-tuple-element.13) | copy-start | bytes 50331652
